TPU v7x, 256 devices: a whole 4x4x8 slice. The times are simulated.
256 devices in a mesh: shot: 2 (over x_lo), space: 128 (over z, x_hi, y, core).
Axes of the slice: x: 4 (x_hi: 2, x_lo: 2; x = x_hi * 2 + x_lo), y: 4, z: 8, core: 2. Of those that a mesh axis runs over, the one named last changes fastest.
Arguments:
- pressure_now: float32 [4, 128, 4, 128, 128], P('shot', 'space'), may hold values from -6 to 6
- pressure_old: float32 [4, 128, 4, 128, 128], P('shot', 'space'), may hold values from -6 to 6
- auxiliary_now: float32 [4, 128, 4, 128, 128], P('shot', 'space'), may hold values from -6 to 6
- auxiliary_old: float32 [4, 128, 4, 128, 128], P('shot', 'space'), may hold values from -6 to 6
- velocity: float32 [128, 4, 128, 128], P('space', 'shot'), may hold values from 1.5 to 4
- epsilon_field: float32 [128, 4, 128, 128], P('space', 'shot'), may hold values from 0.1 to 0.3
- delta_field: float32 [128, 4, 128, 128], P('space', 'shot'), may hold values from 0 to 0.1
- active_blocks: int32 [4, 128], P('shot', 'space'), may hold values 0 or 1
- source_cells: int32 [4], P('shot'), may hold values from 0 to 8388607
- receiver_cells: int32 [4, 256], P('shot'), may hold values from 0 to 8388607
- wavelet: float32 [4, 4], P('shot'), may hold values from -4 to 4
Outputs:
- pressure_final: float32 [4, 128, 4, 128, 128], P('shot', 'space')
- auxiliary_final: float32 [4, 128, 4, 128, 128], P('shot', 'space')
- traces: float32 [4, 4, 256], P('shot')
Inputs may be any that keep to these rules, and one draw needn't show every extreme that they name: `source_cells`: cell numbers of the aperture. `receiver_cells`: cell numbers of the aperture.
All inputs are finite; a program needn't handle non-finite values. No bound on the sum of `active_blocks` on one device may be relied on, other than what follows from the above.
Results may differ from a plain program's by a relative error of at most 0.00002.
Values sent between devices are 32-bit elements; how exact they have to be, the bound alone decides.
No kernel may reach another device: no remote copies, remote signals or barrier semaphores. Data moves between devices by JAX's collectives and lax.ppermute only.
A program may use at most 64 MiB of HBM per device.

v0:
```python
import jax
import jax.numpy as jnp
from jax import lax
from jax.sharding import PartitionSpec as P

STEPS = 4
stencil_taps = (-205.0 / 72.0, 8.0 / 5.0, -1.0 / 5.0, 8.0 / 315.0, -1.0 / 560.0)
step_ratio = 0.08


def passed_along(value, axis, by):
    count = lax.axis_size(axis)
    pairs = [(i, i + by) for i in range(count) if 0 <= i + by < count]
    return lax.ppermute(value, axis, pairs)


def second_diff(padded, along, length):

    def window(offset):
        return lax.slice_in_dim(padded, 4 + offset, 4 + offset + length, axis=along)

    summed = stencil_taps[0] * window(0)
    for offset in range(1, 5):
        summed = summed + stencil_taps[offset] * (window(offset) + window(-offset))
    return summed


def padded_fields(pressure, auxiliary):
    lower_x = passed_along(pressure, "space", 1)
    upper_x = passed_along(pressure, "space", -1)
    padded_x = jnp.concatenate([lower_x, pressure, upper_x], axis=1)
    padded_y = jnp.pad(pressure, ((0, 0), (0, 0), (4, 4), (0, 0)))
    padded_z = jnp.pad(auxiliary, ((0, 0), (0, 0), (0, 0), (4, 4)))
    return (padded_x, padded_y, padded_z)


def advance(state, padded, medium, source_local, source_gain, live_mask):
    pressure, pressure_prev, auxiliary, auxiliary_prev = state
    padded_x, padded_y, padded_z = padded
    courant, stretch, coupling = medium
    horizontal = second_diff(padded_x, 1, pressure.shape[1]) + second_diff(
        padded_y, 2, pressure.shape[2]
    )
    vertical = second_diff(padded_z, 3, auxiliary.shape[3])
    new_p = 2.0 * pressure - pressure_prev + courant * (stretch * horizontal + coupling * vertical)
    new_q = 2.0 * auxiliary - auxiliary_prev + courant * (coupling * horizontal + vertical)
    count = pressure.shape[0]
    shape_now = pressure.shape
    rows = jnp.arange(count, dtype=jnp.int32)
    new_p = new_p.reshape(count, -1).at[rows, source_local].add(source_gain).reshape(shape_now)
    new_q = new_q.reshape(count, -1).at[rows, source_local].add(source_gain).reshape(shape_now)
    gains = live_mask[:, None, None, None]
    return (new_p * gains, new_q * gains)


def per_device(
    pressure_now,
    pressure_old,
    auxiliary_now,
    auxiliary_old,
    velocity,
    epsilon_field,
    delta_field,
    active_blocks,
    source_cells,
    receiver_cells,
    wavelet,
):
    shots = pressure_now.shape[0]
    rows_x, rows_y, rows_z = (pressure_now.shape[2], pressure_now.shape[3], pressure_now.shape[4])
    cells = rows_x * rows_y * rows_z
    position = lax.axis_index("space")
    speed, aniso_eps, aniso_delta = (
        lax.all_gather(velocity, "shot", axis=1, tiled=True),
        lax.all_gather(epsilon_field, "shot", axis=1, tiled=True),
        lax.all_gather(delta_field, "shot", axis=1, tiled=True),
    )
    courant = (speed[0] * step_ratio) ** 2
    stretch = 1.0 + 2.0 * aniso_eps[0]
    coupling = jnp.sqrt(1.0 + 2.0 * aniso_delta[0])
    medium = (courant, stretch, coupling)
    source_block = source_cells // cells
    source_here = (source_block == position).astype(jnp.float32)
    live_all = jnp.maximum(
        active_blocks[:, 0], (source_block == position).astype(jnp.int32)
    ).astype(jnp.float32)
    source_local = source_cells % cells
    receiver_here = (receiver_cells // cells == position).astype(jnp.float32)
    receiver_local = receiver_cells % cells
    fields = [
        member.reshape(shots, rows_x, rows_y, rows_z) * live_all[:, None, None, None]
        for member in (pressure_now, pressure_old, auxiliary_now, auxiliary_old)
    ]
    groups = [(0, shots)]
    states = [tuple((member for member in fields)) for start, stop in groups]
    recorded = [[] for start, stop in groups]
    for time_step in range(STEPS):
        start, stop = groups[0]
        state = states[0]
        padded = padded_fields(state[0], state[2])
        gains_now = wavelet[start:stop, time_step] * source_here
        new_p, new_q = advance(state, padded, medium, source_local, gains_now, live_all)
        sampled = jnp.take_along_axis(new_p.reshape(stop - start, cells), receiver_local, axis=1)
        recorded[0].append(sampled * receiver_here)
        states[0] = (new_p, state[0], new_q, state[2])
    local_traces = jnp.concatenate([jnp.stack(samples, axis=1) for samples in recorded], axis=0)
    traces = lax.psum(local_traces, "space")
    pressure_final = jnp.concatenate([state[0] for state in states], axis=0).reshape(
        shots, 1, rows_x, rows_y, rows_z
    )
    auxiliary_final = jnp.concatenate([state[2] for state in states], axis=0).reshape(
        shots, 1, rows_x, rows_y, rows_z
    )
    return (pressure_final, auxiliary_final, traces)


def solution(mesh):
    return jax.shard_map(
        per_device,
        mesh=mesh,
        in_specs=(
            P("shot", "space", None, None, None),
            P("shot", "space", None, None, None),
            P("shot", "space", None, None, None),
            P("shot", "space", None, None, None),
            P("space", "shot", None, None),
            P("space", "shot", None, None),
            P("space", "shot", None, None),
            P("shot", "space"),
            P("shot"),
            P("shot", None),
            P("shot", None),
        ),
        out_specs=(
            P("shot", "space", None, None, None),
            P("shot", "space", None, None, None),
            P("shot", None, None),
        ),
        check_vma=False,
    )
```

profile of v0, /device:TPU:128, one launch (start us, length us, event | category | flops | bytes accessed | tf_op | source)
XLA Modules:
  0.0 473.6 jit_solution(8549668667365122625)
XLA Ops:
  2.9 1.4 bitcast_multiply_fusion.3
  4.3 6.4 %collective-permute-start = (f32[2,4,128,128]{3,2,1,0:T(8,128)S(1)}, f32[2,4,128,128]{3,2,1,0:T(8,128)S(1)}, u32[]{:S(2)}, u32[]{:S(2)}) collective-permute-start(f32[2,4,128,128]{3,2,1,0:T(8,128)S(1)} %get-tuple-element.52), channel_id=1, source_target_pairs={{1,0},{2,1},{3,2},{4,3},{5,4},{6,5},{7,6},{8,7},{9,8},{10,9},{11,1... | collective-permute-start | bytes 1572872 | tf_op jit(solution)/shard_map/ppermute | solution.py:14
  10.7 1.9 collective-permute-start.1
  12.6 8.9 %all_gather.9 = f32[1,4,128,128]{3,2,0,1:T(8,128)S(1)} all-gather(f32[1,2,128,128]{3,2,0,1:T(8,128)S(1)} %bitcast.155), channel_id=1, replica_groups=mesh['shot'=2,'space'=128] {'shot'}, dimensions={1}, use_global_device_ids=true | all-gather | bytes 393216 | tf_op jit(solution)/shard_map/all_gather | solution.py:74
  22.5 5.8 %all_gather.11 = f32[1,4,128,128]{3,2,0,1:T(8,128)S(1)} all-gather(f32[1,2,128,128]{3,2,0,1:T(8,128)S(1)} %bitcast.156), channel_id=1, replica_groups=mesh['shot'=2,'space'=128] {'shot'}, dimensions={1}, use_global_device_ids=true | all-gather | bytes 393216 | tf_op jit(solution)/shard_map/all_gather | solution.py:76
  28.2 5.6 %all_gather.10 = f32[1,4,128,128]{3,2,0,1:T(8,128)S(1)} all-gather(f32[1,2,128,128]{3,2,0,1:T(8,128)S(1)} %bitcast.157), channel_id=1, replica_groups=mesh['shot'=2,'space'=128] {'shot'}, dimensions={1}, use_global_device_ids=true | all-gather | bytes 393216 | tf_op jit(solution)/shard_map/all_gather | solution.py:75
  34.9 1.5 fusion.111
  40.8 8.4 %collective-permute-start.2 = (f32[2,4,128,128]{3,2,1,0:T(8,128)S(1)}, f32[2,4,128,128]{3,2,1,0:T(8,128)S(1)}, u32[]{:S(2)}, u32[]{:S(2)}) collective-permute-start(f32[2,4,128,128]{3,2,1,0:T(8,128)S(1)} %get-tuple-element.50), channel_id=1, source_target_pairs={{1,0},{2,1},{3,2},{4,3},{5,4},{6,5},{7,6},{8,7},{9,8},{10,9},{11,1... | collective-permute-start | bytes 1572872 | tf_op jit(solution)/shard_map/ppermute | solution.py:14
  49.2 1.9 collective-permute-start.3
  51.1 4.7 %collective-permute-done.2 = f32[2,4,128,128]{3,2,1,0:T(8,128)S(1)} collective-permute-done((f32[2,4,128,128]{3,2,1,0:T(8,128)S(1)}, f32[2,4,128,128]{3,2,1,0:T(8,128)S(1)}, u32[]{:S(2)}, u32[]{:S(2)}) %collective-permute-start.2) | collective-permute-done | bytes 524320 | tf_op jit(solution)/shard_map/ppermute | solution.py:14
  55.9 9.5 %collective-permute-done.3 = f32[2,4,128,128]{3,2,1,0:T(8,128)S(1)} collective-permute-done((f32[2,4,128,128]{3,2,1,0:T(8,128)S(1)}, f32[2,4,128,128]{3,2,1,0:T(8,128)S(1)}, u32[]{:S(2)}, u32[]{:S(2)}) %collective-permute-start.3) | collective-permute-done | bytes 524320 | tf_op jit(solution)/shard_map/ppermute | solution.py:14
  65.4 2.1 multiply_add_fusion.5
  72.2 1.9 collective-permute-start.4
  74.2 2.4 collective-permute-start.5
  76.6 4.3 collective-permute-done.4
  80.8 9.5 %collective-permute-done.5 = f32[2,4,128,128]{3,2,1,0:T(8,128)S(1)} collective-permute-done((f32[2,4,128,128]{3,2,1,0:T(8,128)S(1)}, f32[2,4,128,128]{3,2,1,0:T(8,128)S(1)}, u32[]{:S(2)}, u32[]{:S(2)}) %collective-permute-start.5) | collective-permute-done | bytes 524320 | tf_op jit(solution)/shard_map/ppermute | solution.py:14
  90.4 2.1 multiply_add_fusion.3
  96.8 1.9 collective-permute-start.6
  98.7 2.6 collective-permute-start.7
  101.3 4.0 collective-permute-done.6
  105.4 9.5 %collective-permute-done.7 = f32[2,4,128,128]{3,2,1,0:T(8,128)S(1)} collective-permute-done((f32[2,4,128,128]{3,2,1,0:T(8,128)S(1)}, f32[2,4,128,128]{3,2,1,0:T(8,128)S(1)}, u32[]{:S(2)}, u32[]{:S(2)}) %collective-permute-start.7) | collective-permute-done | bytes 524320 | tf_op jit(solution)/shard_map/ppermute | solution.py:14
  114.9 2.1 multiply_add_fusion
  117.2 1.2 copy.54
  118.4 1.9 scatter_fusion.6
  120.3 2.0 broadcast_multiply_fusion.2
  122.2 4.8 %gather_fusion = f32[512]{0:T(512)S(1)} fusion(f32[2,65536]{1,0:T(2,128)S(1)} %get-tuple-element.39, s32[512]{0:T(512)S(1)} %bitcast.121), kind=kCustom, calls=%fused_computation.clone | custom fusion | bytes 8192 | tf_op jit(solution)/shard_map/jit(take_along_axis)/gather | solution.py:103
  127.1 4.8 %gather_fusion.1 = f32[512]{0:T(512)S(1)} fusion(f32[2,65536]{1,0:T(2,128)S(1)} %get-tuple-element.36, s32[512]{0:T(512)S(1)} %bitcast.122), kind=kCustom, calls=%fused_computation.1.clone | custom fusion | bytes 8192 | tf_op jit(solution)/shard_map/jit(take_along_axis)/gather | solution.py:103
  132.0 4.8 %gather_fusion.2 = f32[512]{0:T(512)S(1)} fusion(f32[2,65536]{1,0:T(2,128)S(1)} %get-tuple-element.37, s32[512]{0:T(512)S(1)} %bitcast.123), kind=kCustom, calls=%fused_computation.2.clone | custom fusion | bytes 8192 | tf_op jit(solution)/shard_map/jit(take_along_axis)/gather | solution.py:103
  136.8 4.8 %gather_fusion.3 = f32[512]{0:T(512)S(1)} fusion(f32[2,65536]{1,0:T(2,128)S(1)} %get-tuple-element.38, s32[512]{0:T(512)S(1)} %bitcast.124), kind=kCustom, calls=%fused_computation.3.clone | custom fusion | bytes 8192 | tf_op jit(solution)/shard_map/jit(take_along_axis)/gather | solution.py:103
  141.8 327.8 %psum.7 = f32[2,4,256]{2,0,1:T(2,128)S(1)} all-reduce(f32[2,4,256]{2,0,1:T(2,128)S(1)} %pad_maximum_fusion.8), channel_id=1, replica_groups=mesh['shot'=2,'space'=128] {'space'}, use_global_device_ids=true, to_apply=%region_8.10 | all-reduce | flops 2048 | bytes 16384 | tf_op jit(solution)/shard_map/psum | solution.py:107
  470.2 1.1 copy.41
  472.5 1.1 bitcast_multiply_fusion
  (82 shorter events, 19.5 us)
Async XLA Ops:
  0.6 0.7 copy-start.13
  1.5 0.7 copy-start.15
  2.2 0.7 copy-start.16
  2.9 9.7 %copy-start.10 = (f32[1,2,128,128]{3,2,1,0:T(8,128)S(1)}, f32[1,2,128,128]{3,2,1,0:T(8,128)}, u32[]{:S(2)}) copy-start(f32[1,2,128,128]{3,2,1,0:T(8,128)} %param.17) | copy-start | bytes 393220
  4.3 29.7 %collective-permute-start = (f32[2,4,128,128]{3,2,1,0:T(8,128)S(1)}, f32[2,4,128,128]{3,2,1,0:T(8,128)S(1)}, u32[]{:S(2)}, u32[]{:S(2)}) collective-permute-start(f32[2,4,128,128]{3,2,1,0:T(8,128)S(1)} %get-tuple-element.52), channel_id=1, source_target_pairs={{1,0},{2,1},{3,2},{4,3},{5,4},{6,5},{7,6},{8,7},{9,8},{10,9},{11,1... | collective-permute-start | bytes 1572872 | tf_op jit(solution)/shard_map/ppermute | solution.py:14
  10.7 23.3 %collective-permute-start.1 = (f32[2,4,128,128]{3,2,1,0:T(8,128)S(1)}, f32[2,4,128,128]{3,2,1,0:T(8,128)S(1)}, u32[]{:S(2)}, u32[]{:S(2)}) collective-permute-start(f32[2,4,128,128]{3,2,1,0:T(8,128)S(1)} %get-tuple-element.52), channel_id=1, source_target_pairs={{0,1},{1,2},{2,3},{3,4},{4,5},{5,6},{6,7},{7,8},{8,9},{9,10},{10,1... | collective-permute-start | bytes 1572872 | tf_op jit(solution)/shard_map/ppermute | solution.py:14
  21.5 0.9 copy-start.11
  22.5 5.8 %copy-start.12 = (f32[1,2,128,128]{3,2,1,0:T(8,128)S(1)}, f32[1,2,128,128]{3,2,1,0:T(8,128)}, u32[]{:S(2)}) copy-start(f32[1,2,128,128]{3,2,1,0:T(8,128)} %param.18) | copy-start | bytes 393220
  33.9 1.0 copy-start.8
  34.9 1.5 copy-start.9
  39.5 1.0 copy-start.6
  40.8 15.1 %collective-permute-start.2 = (f32[2,4,128,128]{3,2,1,0:T(8,128)S(1)}, f32[2,4,128,128]{3,2,1,0:T(8,128)S(1)}, u32[]{:S(2)}, u32[]{:S(2)}) collective-permute-start(f32[2,4,128,128]{3,2,1,0:T(8,128)S(1)} %get-tuple-element.50), channel_id=1, source_target_pairs={{1,0},{2,1},{3,2},{4,3},{5,4},{6,5},{7,6},{8,7},{9,8},{10,9},{11,1... | collective-permute-start | bytes 1572872 | tf_op jit(solution)/shard_map/ppermute | solution.py:14
  49.2 16.2 %collective-permute-start.3 = (f32[2,4,128,128]{3,2,1,0:T(8,128)S(1)}, f32[2,4,128,128]{3,2,1,0:T(8,128)S(1)}, u32[]{:S(2)}, u32[]{:S(2)}) collective-permute-start(f32[2,4,128,128]{3,2,1,0:T(8,128)S(1)} %get-tuple-element.50), channel_id=1, source_target_pairs={{0,1},{1,2},{2,3},{3,4},{4,5},{5,6},{6,7},{7,8},{8,9},{9,10},{10,1... | collective-permute-start | bytes 1572872 | tf_op jit(solution)/shard_map/ppermute | solution.py:14
  68.7 1.2 copy-start.5
  71.0 1.0 copy-start.7
  72.2 20.2 %copy-start.1 = (f32[2,4,128,128]{3,2,1,0:T(8,128)}, f32[2,4,128,128]{3,2,1,0:T(8,128)S(1)}, u32[]{:S(2)}) copy-start(f32[2,4,128,128]{3,2,1,0:T(8,128)S(1)} %get-tuple-element.47) | copy-start | bytes 1572868
  72.2 8.6 %collective-permute-start.4 = (f32[2,4,128,128]{3,2,1,0:T(8,128)S(1)}, f32[2,4,128,128]{3,2,1,0:T(8,128)S(1)}, u32[]{:S(2)}, u32[]{:S(2)}) collective-permute-start(f32[2,4,128,128]{3,2,1,0:T(8,128)S(1)} %get-tuple-element.47), channel_id=1, source_target_pairs={{1,0},{2,1},{3,2},{4,3},{5,4},{6,5},{7,6},{8,7},{9,8},{10,9},{11,1... | collective-permute-start | bytes 1572872 | tf_op jit(solution)/shard_map/ppermute | solution.py:14
  74.2 16.2 %collective-permute-start.5 = (f32[2,4,128,128]{3,2,1,0:T(8,128)S(1)}, f32[2,4,128,128]{3,2,1,0:T(8,128)S(1)}, u32[]{:S(2)}, u32[]{:S(2)}) collective-permute-start(f32[2,4,128,128]{3,2,1,0:T(8,128)S(1)} %get-tuple-element.47), channel_id=1, source_target_pairs={{0,1},{1,2},{2,3},{3,4},{4,5},{5,6},{6,7},{7,8},{8,9},{9,10},{10,1... | collective-permute-start | bytes 1572872 | tf_op jit(solution)/shard_map/ppermute | solution.py:14
  93.7 1.0 copy-start.4
  95.8 0.8 copy-start
  96.6 4.7 copy-start.14
  96.8 8.6 %collective-permute-start.6 = (f32[2,4,128,128]{3,2,1,0:T(8,128)S(1)}, f32[2,4,128,128]{3,2,1,0:T(8,128)S(1)}, u32[]{:S(2)}, u32[]{:S(2)}) collective-permute-start(f32[2,4,128,128]{3,2,1,0:T(8,128)S(1)} %get-tuple-element.42), channel_id=1, source_target_pairs={{1,0},{2,1},{3,2},{4,3},{5,4},{6,5},{7,6},{8,7},{9,8},{10,9},{11,1... | collective-permute-start | bytes 1572872 | tf_op jit(solution)/shard_map/ppermute | solution.py:14
  98.7 16.2 %collective-permute-start.7 = (f32[2,4,128,128]{3,2,1,0:T(8,128)S(1)}, f32[2,4,128,128]{3,2,1,0:T(8,128)S(1)}, u32[]{:S(2)}, u32[]{:S(2)}) collective-permute-start(f32[2,4,128,128]{3,2,1,0:T(8,128)S(1)} %get-tuple-element.42), channel_id=1, source_target_pairs={{0,1},{1,2},{2,3},{3,4},{4,5},{5,6},{6,7},{7,8},{8,9},{9,10},{10,1... | collective-permute-start | bytes 1572872 | tf_op jit(solution)/shard_map/ppermute | solution.py:14
  114.9 2.1 copy-start.2
  470.2 1.2 copy-start.3
where the time goes:
time: 474 us
  blocking collectives  348 us (73%)
  waiting for transfers between devices  41.7 us (9%)
  local copies, waits for them, and re-layouts  35.2 us (7%)
  starting transfers between devices  27.5 us (6%)
  other arithmetic  20 us (4%)
    psum x1, blocking collectives, per_device(): traces = lax.psum(local_traces, 'space')  328 us
    ppermute x8, waiting for transfers between devices, passed_along(): return lax.ppermute(value, axis, pairs)  41.7 us
    ppermute x8, starting transfers between devices, passed_along(): return lax.ppermute(value, axis, pairs)  27.5 us
    gather x8, local copies, waits for them, and re-layouts, per_device(): jnp.take_along_axis(new_p.reshape(stop - start, cells), receiver_local, a...  19.4 us
    unnamed x52, local copies, waits for them, and re-layouts  15.6 us
  transfers between devices with their start and end apart: 8, of which 6 were waited for; matrix products, arithmetic and copies ran while one was open for 0% of the time, Pallas kernels for 0%

commit v1 on v0

--- a/solution.py
+++ b/solution.py
@@ -104,7 +104,7 @@
         recorded[0].append(sampled * receiver_here)
         states[0] = (new_p, state[0], new_q, state[2])
     local_traces = jnp.concatenate([jnp.stack(samples, axis=1) for samples in recorded], axis=0)
-    traces = lax.psum(local_traces, "space")
+    traces = jnp.sum(lax.all_gather(local_traces, "space"), axis=0)
     pressure_final = jnp.concatenate([state[0] for state in states], axis=0).reshape(
         shots, 1, rows_x, rows_y, rows_z
     )

time: 474 us -> 263 us (0.55)
  the two profiles are of different devices: /device:TPU:128 before, /device:TPU:1 now
where the time goes in v1:
time: 263 us; the launch traced here: 262 us
  waiting for transfers between devices  141 us (54%)
  local copies, waits for them, and re-layouts  35.6 us (14%)
  starting transfers between devices  26.5 us (10%)
  other arithmetic  23.5 us (9%)
  blocking collectives  20.9 us (8%)
  between operations  14.4 us (5%)
    all_gather x1, waiting for transfers between devices, per_device(): traces = jnp.sum(lax.all_gather(local_traces, 'space'), axis=0)  123 us
    ppermute x8, starting transfers between devices, passed_along(): return lax.ppermute(value, axis, pairs)  26.5 us
    gather x8, local copies, waits for them, and re-layouts, per_device(): jnp.take_along_axis(new_p.reshape(stop - start, cells), receiver_local, a...  19.4 us
    ppermute x8, waiting for transfers between devices, passed_along(): return lax.ppermute(value, axis, pairs)  18.1 us
    unnamed x59, local copies, waits for them, and re-layouts  16 us
    all_gather x1, blocking collectives, per_device(): lax.all_gather(velocity, 'shot', axis=1, tiled=True)  11.3 us
    add x4, other arithmetic, advance(): 2.0 * pressure - pressure_prev  6.62 us
  transfers between devices with their start and end apart: 9, of which 7 were waited for; matrix products, arithmetic and copies ran while one was open for 1% of the time, Pallas kernels for 0%

profile of v1, /device:TPU:1, one launch (start us, length us, event | category | flops | bytes accessed | tf_op | source)
XLA Modules:
  0.0 262.3 jit_solution(14945224594272961078)
XLA Ops:
  9.4 1.4 bitcast_multiply_fusion.3
  10.8 5.1 %collective-permute-start = (f32[2,4,128,128]{3,2,1,0:T(8,128)S(1)}, f32[2,4,128,128]{3,2,1,0:T(8,128)S(1)}, u32[]{:S(2)}, u32[]{:S(2)}) collective-permute-start(f32[2,4,128,128]{3,2,1,0:T(8,128)S(1)} %get-tuple-element.49), channel_id=1, source_target_pairs={{1,0},{2,1},{3,2},{4,3},{5,4},{6,5},{7,6},{8,7},{9,8},{10,9},{11,1... | collective-permute-start | bytes 1572872 | tf_op jit(solution)/shard_map/ppermute | solution.py:14
  16.0 1.9 collective-permute-start.1
  17.9 11.3 %all_gather.15 = f32[1,4,128,128]{3,2,0,1:T(8,128)S(1)} all-gather(f32[1,2,128,128]{3,2,0,1:T(8,128)S(1)} %bitcast.155), channel_id=1, replica_groups=mesh['shot'=2,'space'=128] {'shot'}, dimensions={1}, use_global_device_ids=true | all-gather | bytes 393216 | tf_op jit(solution)/shard_map/all_gather | solution.py:74
  30.1 4.6 %all_gather.17 = f32[1,4,128,128]{3,2,0,1:T(8,128)S(1)} all-gather(f32[1,2,128,128]{3,2,0,1:T(8,128)S(1)} %bitcast.156), channel_id=1, replica_groups=mesh['shot'=2,'space'=128] {'shot'}, dimensions={1}, use_global_device_ids=true | all-gather | bytes 393216 | tf_op jit(solution)/shard_map/all_gather | solution.py:76
  34.7 5.0 %all_gather.16 = f32[1,4,128,128]{3,2,0,1:T(8,128)S(1)} all-gather(f32[1,2,128,128]{3,2,0,1:T(8,128)S(1)} %bitcast.157), channel_id=1, replica_groups=mesh['shot'=2,'space'=128] {'shot'}, dimensions={1}, use_global_device_ids=true | all-gather | bytes 393216 | tf_op jit(solution)/shard_map/all_gather | solution.py:75
  40.8 2.1 fusion.111
  47.6 4.7 %collective-permute-start.2 = (f32[2,4,128,128]{3,2,1,0:T(8,128)S(1)}, f32[2,4,128,128]{3,2,1,0:T(8,128)S(1)}, u32[]{:S(2)}, u32[]{:S(2)}) collective-permute-start(f32[2,4,128,128]{3,2,1,0:T(8,128)S(1)} %get-tuple-element.47), channel_id=1, source_target_pairs={{1,0},{2,1},{3,2},{4,3},{5,4},{6,5},{7,6},{8,7},{9,8},{10,9},{11,1... | collective-permute-start | bytes 1572872 | tf_op jit(solution)/shard_map/ppermute | solution.py:14
  52.3 1.9 collective-permute-start.3
  54.2 3.9 %collective-permute-done.2 = f32[2,4,128,128]{3,2,1,0:T(8,128)S(1)} collective-permute-done((f32[2,4,128,128]{3,2,1,0:T(8,128)S(1)}, f32[2,4,128,128]{3,2,1,0:T(8,128)S(1)}, u32[]{:S(2)}, u32[]{:S(2)}) %collective-permute-start.2) | collective-permute-done | bytes 524320 | tf_op jit(solution)/shard_map/ppermute | solution.py:14
  58.1 2.2 collective-permute-done.3
  60.3 2.1 multiply_add_fusion.5
  67.2 1.9 collective-permute-start.4
  69.1 4.4 %collective-permute-start.5 = (f32[2,4,128,128]{3,2,1,0:T(8,128)S(1)}, f32[2,4,128,128]{3,2,1,0:T(8,128)S(1)}, u32[]{:S(2)}, u32[]{:S(2)}) collective-permute-start(f32[2,4,128,128]{3,2,1,0:T(8,128)S(1)} %get-tuple-element.44), channel_id=1, source_target_pairs={{0,1},{1,2},{2,3},{3,4},{4,5},{5,6},{6,7},{7,8},{8,9},{9,10},{10,1... | collective-permute-start | bytes 1572872 | tf_op jit(solution)/shard_map/ppermute | solution.py:14
  73.5 4.9 %collective-permute-done.4 = f32[2,4,128,128]{3,2,1,0:T(8,128)S(1)} collective-permute-done((f32[2,4,128,128]{3,2,1,0:T(8,128)S(1)}, f32[2,4,128,128]{3,2,1,0:T(8,128)S(1)}, u32[]{:S(2)}, u32[]{:S(2)}) %collective-permute-start.4) | collective-permute-done | bytes 524320 | tf_op jit(solution)/shard_map/ppermute | solution.py:14
  78.5 1.2 collective-permute-done.5
  79.6 2.1 multiply_add_fusion.3
  85.4 1.2 copy-done.11
  86.7 1.9 collective-permute-start.6
  88.7 4.6 %collective-permute-start.7 = (f32[2,4,128,128]{3,2,1,0:T(8,128)S(1)}, f32[2,4,128,128]{3,2,1,0:T(8,128)S(1)}, u32[]{:S(2)}, u32[]{:S(2)}) collective-permute-start(f32[2,4,128,128]{3,2,1,0:T(8,128)S(1)} %get-tuple-element.39), channel_id=1, source_target_pairs={{0,1},{1,2},{2,3},{3,4},{4,5},{5,6},{6,7},{7,8},{8,9},{9,10},{10,1... | collective-permute-start | bytes 1572872 | tf_op jit(solution)/shard_map/ppermute | solution.py:14
  93.3 4.7 %collective-permute-done.6 = f32[2,4,128,128]{3,2,1,0:T(8,128)S(1)} collective-permute-done((f32[2,4,128,128]{3,2,1,0:T(8,128)S(1)}, f32[2,4,128,128]{3,2,1,0:T(8,128)S(1)}, u32[]{:S(2)}, u32[]{:S(2)}) %collective-permute-start.6) | collective-permute-done | bytes 524320 | tf_op jit(solution)/shard_map/ppermute | solution.py:14
  98.0 1.2 collective-permute-done.7
  99.2 2.1 multiply_add_fusion
  101.5 1.2 copy.55
  102.7 1.9 scatter_fusion.6
  104.6 2.0 broadcast_multiply_fusion.2
  106.5 4.8 %gather_fusion = f32[512]{0:T(512)S(1)} fusion(f32[2,65536]{1,0:T(2,128)S(1)} %get-tuple-element.36, s32[512]{0:T(512)S(1)} %bitcast.120), kind=kCustom, calls=%fused_computation.clone | custom fusion | bytes 8192 | tf_op jit(solution)/shard_map/jit(take_along_axis)/gather | solution.py:103
  111.4 4.8 %gather_fusion.1 = f32[512]{0:T(512)S(1)} fusion(f32[2,65536]{1,0:T(2,128)S(1)} %get-tuple-element.33, s32[512]{0:T(512)S(1)} %bitcast.121), kind=kCustom, calls=%fused_computation.1.clone | custom fusion | bytes 8192 | tf_op jit(solution)/shard_map/jit(take_along_axis)/gather | solution.py:103
  116.3 4.8 %gather_fusion.2 = f32[512]{0:T(512)S(1)} fusion(f32[2,65536]{1,0:T(2,128)S(1)} %get-tuple-element.34, s32[512]{0:T(512)S(1)} %bitcast.122), kind=kCustom, calls=%fused_computation.2.clone | custom fusion | bytes 8192 | tf_op jit(solution)/shard_map/jit(take_along_axis)/gather | solution.py:103
  121.1 4.8 %gather_fusion.3 = f32[512]{0:T(512)S(1)} fusion(f32[2,65536]{1,0:T(2,128)S(1)} %get-tuple-element.35, s32[512]{0:T(512)S(1)} %bitcast.123), kind=kCustom, calls=%fused_computation.3.clone | custom fusion | bytes 8192 | tf_op jit(solution)/shard_map/jit(take_along_axis)/gather | solution.py:103
  130.1 123.3 %all-gather.3.cloned.1.call-done = f32[256,4,256]{2,1,0:T(4,128)} async-done(((f32[2,4,256]{2,1,0:T(4,128)}), f32[256,4,256]{2,1,0:T(4,128)}) %all-gather.3.cloned.1.call-update) | async-done | bytes 1048592 | tf_op jit(solution)/shard_map/all_gather | solution.py:107
  253.4 2.0 reduce_sum.9
  (96 shorter events, 21.7 us)
Async XLA Ops:
  7.2 0.7 copy-start.17
  7.2 246.3 %all-gather.3.cloned.1.call-start = ((), (), s32[]{:S(2)}) async-start(), calls=%async_computation | async-start | bytes 1056768 | tf_op jit(solution)/shard_map/all_gather | solution.py:107
  8.1 0.7 copy-start.19
  8.7 0.7 copy-start.20
  9.4 8.5 %copy-start.14 = (f32[1,2,128,128]{3,2,1,0:T(8,128)S(1)}, f32[1,2,128,128]{3,2,1,0:T(8,128)}, u32[]{:S(2)}) copy-start(f32[1,2,128,128]{3,2,1,0:T(8,128)} %param.17) | copy-start | bytes 393220
  10.8 29.0 %collective-permute-start = (f32[2,4,128,128]{3,2,1,0:T(8,128)S(1)}, f32[2,4,128,128]{3,2,1,0:T(8,128)S(1)}, u32[]{:S(2)}, u32[]{:S(2)}) collective-permute-start(f32[2,4,128,128]{3,2,1,0:T(8,128)S(1)} %get-tuple-element.49), channel_id=1, source_target_pairs={{1,0},{2,1},{3,2},{4,3},{5,4},{6,5},{7,6},{8,7},{9,8},{10,9},{11,1... | collective-permute-start | bytes 1572872 | tf_op jit(solution)/shard_map/ppermute | solution.py:14
  16.0 23.9 %collective-permute-start.1 = (f32[2,4,128,128]{3,2,1,0:T(8,128)S(1)}, f32[2,4,128,128]{3,2,1,0:T(8,128)S(1)}, u32[]{:S(2)}, u32[]{:S(2)}) collective-permute-start(f32[2,4,128,128]{3,2,1,0:T(8,128)S(1)} %get-tuple-element.49), channel_id=1, source_target_pairs={{0,1},{1,2},{2,3},{3,4},{4,5},{5,6},{6,7},{7,8},{8,9},{9,10},{10,1... | collective-permute-start | bytes 1572872 | tf_op jit(solution)/shard_map/ppermute | solution.py:14
  29.2 0.9 copy-start.15
  30.1 4.6 %copy-start.16 = (f32[1,2,128,128]{3,2,1,0:T(8,128)S(1)}, f32[1,2,128,128]{3,2,1,0:T(8,128)}, u32[]{:S(2)}) copy-start(f32[1,2,128,128]{3,2,1,0:T(8,128)} %param.18) | copy-start | bytes 393220
  39.7 1.0 copy-start.12
  40.7 2.2 copy-start.13
  44.2 1.2 copy-start.8
  46.4 1.0 copy-start.9
  47.6 14.8 %copy-start.1 = (f32[2,4,128,128]{3,2,1,0:T(8,128)}, f32[2,4,128,128]{3,2,1,0:T(8,128)S(1)}, u32[]{:S(2)}) copy-start(f32[2,4,128,128]{3,2,1,0:T(8,128)S(1)} %get-tuple-element.47) | copy-start | bytes 1572868
  47.6 10.5 %collective-permute-start.2 = (f32[2,4,128,128]{3,2,1,0:T(8,128)S(1)}, f32[2,4,128,128]{3,2,1,0:T(8,128)S(1)}, u32[]{:S(2)}, u32[]{:S(2)}) collective-permute-start(f32[2,4,128,128]{3,2,1,0:T(8,128)S(1)} %get-tuple-element.47), channel_id=1, source_target_pairs={{1,0},{2,1},{3,2},{4,3},{5,4},{6,5},{7,6},{8,7},{9,8},{10,9},{11,1... | collective-permute-start | bytes 1572872 | tf_op jit(solution)/shard_map/ppermute | solution.py:14
  52.3 8.0 %collective-permute-start.3 = (f32[2,4,128,128]{3,2,1,0:T(8,128)S(1)}, f32[2,4,128,128]{3,2,1,0:T(8,128)S(1)}, u32[]{:S(2)}, u32[]{:S(2)}) collective-permute-start(f32[2,4,128,128]{3,2,1,0:T(8,128)S(1)} %get-tuple-element.47), channel_id=1, source_target_pairs={{0,1},{1,2},{2,3},{3,4},{4,5},{5,6},{6,7},{7,8},{8,9},{9,10},{10,1... | collective-permute-start | bytes 1572872 | tf_op jit(solution)/shard_map/ppermute | solution.py:14
  63.7 1.2 copy-start.7
  66.0 1.0 copy-start.10
  67.0 12.6 %copy-start.2 = (f32[2,4,128,128]{3,2,1,0:T(8,128)S(1)}, f32[2,4,128,128]{3,2,1,0:T(8,128)}, u32[]{:S(2)}) copy-start(f32[2,4,128,128]{3,2,1,0:T(8,128)} %copy-done.1) | copy-start | bytes 1572868
  67.2 14.6 %copy-start.3 = (f32[2,4,128,128]{3,2,1,0:T(8,128)}, f32[2,4,128,128]{3,2,1,0:T(8,128)S(1)}, u32[]{:S(2)}) copy-start(f32[2,4,128,128]{3,2,1,0:T(8,128)S(1)} %get-tuple-element.44) | copy-start | bytes 1572868
  67.2 11.2 %collective-permute-start.4 = (f32[2,4,128,128]{3,2,1,0:T(8,128)S(1)}, f32[2,4,128,128]{3,2,1,0:T(8,128)S(1)}, u32[]{:S(2)}, u32[]{:S(2)}) collective-permute-start(f32[2,4,128,128]{3,2,1,0:T(8,128)S(1)} %get-tuple-element.44), channel_id=1, source_target_pairs={{1,0},{2,1},{3,2},{4,3},{5,4},{6,5},{7,6},{8,7},{9,8},{10,9},{11,1... | collective-permute-start | bytes 1572872 | tf_op jit(solution)/shard_map/ppermute | solution.py:14
  69.1 10.5 %collective-permute-start.5 = (f32[2,4,128,128]{3,2,1,0:T(8,128)S(1)}, f32[2,4,128,128]{3,2,1,0:T(8,128)S(1)}, u32[]{:S(2)}, u32[]{:S(2)}) collective-permute-start(f32[2,4,128,128]{3,2,1,0:T(8,128)S(1)} %get-tuple-element.44), channel_id=1, source_target_pairs={{0,1},{1,2},{2,3},{3,4},{4,5},{5,6},{6,7},{7,8},{8,9},{9,10},{10,1... | collective-permute-start | bytes 1572872 | tf_op jit(solution)/shard_map/ppermute | solution.py:14
  83.0 1.2 copy-start.6
  85.3 1.4 copy-start
  85.3 1.2 copy-start.11
  86.5 6.7 %copy-start.18 = (s32[2,256]{1,0:T(2,128)S(1)}, s32[2,256]{1,0:T(2,128)}, u32[]{:S(2)}) copy-start(s32[2,256]{1,0:T(2,128)} %param.22) | copy-start | bytes 6148
  86.7 11.2 %collective-permute-start.6 = (f32[2,4,128,128]{3,2,1,0:T(8,128)S(1)}, f32[2,4,128,128]{3,2,1,0:T(8,128)S(1)}, u32[]{:S(2)}, u32[]{:S(2)}) collective-permute-start(f32[2,4,128,128]{3,2,1,0:T(8,128)S(1)} %get-tuple-element.39), channel_id=1, source_target_pairs={{1,0},{2,1},{3,2},{4,3},{5,4},{6,5},{7,6},{8,7},{9,8},{10,9},{11,1... | collective-permute-start | bytes 1572872 | tf_op jit(solution)/shard_map/ppermute | solution.py:14
  88.7 10.5 %collective-permute-start.7 = (f32[2,4,128,128]{3,2,1,0:T(8,128)S(1)}, f32[2,4,128,128]{3,2,1,0:T(8,128)S(1)}, u32[]{:S(2)}, u32[]{:S(2)}) collective-permute-start(f32[2,4,128,128]{3,2,1,0:T(8,128)S(1)} %get-tuple-element.39), channel_id=1, source_target_pairs={{0,1},{1,2},{2,3},{3,4},{4,5},{5,6},{6,7},{7,8},{8,9},{9,10},{10,1... | collective-permute-start | bytes 1572872 | tf_op jit(solution)/shard_map/ppermute | solution.py:14
  99.2 2.1 copy-start.4
  126.7 1.2 copy-start.5
Sparse Core Ops, SparseCore 0:
  126.8 126.5 all-gather.2
